TPU v7x, 32 devices: a whole 2x2x4 slice. The times are simulated.
32 devices in a mesh: rep: 8 (over z, y), tp: 4 (over x, core).
Axes of the slice: x: 2, y: 2, z: 4, core: 2. Of those that a mesh axis runs over, the one named last changes fastest.
Arguments:
- image_grads: bfloat16 [32, 48, 1280], P('rep', 'tp'), may hold values from -6 to 6
- dest_rank: int32 [32], P('rep'), may hold values from 0 to 7, as said below
- dest_slot: int32 [32], P('rep'), may hold values from 0 to 7, as said below
- saved_inputs: bfloat16 [64, 48, 1280], P('rep'), may hold values from -6 to 6
- up_weight: bfloat16 [1280, 5120], P(None, 'tp'), may hold values from -0.15625 to 0.15625
- down_weight: bfloat16 [5120, 1280], P('tp'), may hold values from -0.078125 to 0.078125
- norm_gain: float32 [1280], replicated, may hold values from 0.25 to 1.75
Outputs:
- input_grads: bfloat16 [64, 48, 1280], P('rep', 'tp')
- up_grads: float32 [1280, 5120], P('rep', 'tp')
- down_grads: float32 [5120, 1280], P('tp', 'rep')
- gain_grads: float32 [1280], replicated
Inputs may be any that keep to these rules, and one draw needn't show every extreme that they name: `dest_rank`: the images of one index of rep go to different owners; each owner receives at most 8 images, and some owner receives exactly 8 in every draw. `dest_slot`: the images that one owner receives have distinct slots 0, 1, ... up to their count less one; other slots hold no image.
All inputs are finite; a program needn't handle non-finite values.
Results may differ from a plain program's by a relative error of at most 0.015.
Values may be sent and summed in bfloat16 or wider, within the bound.
No kernel may reach another device: no remote copies, remote signals or barrier semaphores. Data moves between devices by JAX's collectives and lax.ppermute only.
A program may use at most 128 MiB of HBM per device.

v0:
```python
import jax
import jax.numpy as jnp
from jax import lax
from jax.sharding import PartitionSpec as P

epsilon = 1e-05
gelu_c = 0.7978845608028654
gelu_a = 0.044715


def gelu_value(preact):
    inner = jnp.tanh(gelu_c * (preact + gelu_a * preact**3))
    return 0.5 * preact * (1.0 + inner)


def gelu_slope(preact):
    inner = jnp.tanh(gelu_c * (preact + gelu_a * preact**3))
    return 0.5 * (1.0 + inner) + 0.5 * preact * (1.0 - inner * inner) * gelu_c * (
        1.0 + 3.0 * gelu_a * preact * preact
    )


def outbound(images, dest_rank, dest_slot, groups, capacity):
    rank_ids = jnp.arange(groups, dtype=jnp.int32)
    one_hot = dest_rank[None, :] == rank_ids[:, None]
    packed = jnp.einsum(
        "ek,kpd->epd", one_hot.astype(jnp.bfloat16), images, preferred_element_type=jnp.float32
    ).astype(jnp.bfloat16)
    present = jnp.any(one_hot, axis=1)
    slot_sent = jnp.sum(jnp.where(one_hot, dest_slot[None, :], 0), axis=1) + jnp.where(
        present, 0, capacity
    )
    return (packed, slot_sent)


def compact(inbound, slot_recv, capacity):
    slot_ids = jnp.arange(capacity, dtype=jnp.int32)
    picker = (slot_recv[None, :] == slot_ids[:, None]).astype(jnp.bfloat16)
    return jnp.einsum("ce,epd->cpd", picker, inbound, preferred_element_type=jnp.float32).astype(
        jnp.bfloat16
    )


def local(image_grads, dest_rank, dest_slot, saved_inputs, up_weight, down_weight, norm_gain):
    groups = lax.axis_size("rep")
    capacity = saved_inputs.shape[0]
    patches = saved_inputs.shape[1]
    width = saved_inputs.shape[2]
    slab = image_grads.shape[1]
    packed, slot_sent = outbound(image_grads, dest_rank, dest_slot, groups, capacity)
    inbound, slot_recv = (
        lax.all_to_all(packed, "rep", split_axis=0, concat_axis=0, tiled=True),
        lax.all_to_all(slot_sent, "rep", split_axis=0, concat_axis=0, tiled=True),
    )
    routed = lax.all_gather(compact(inbound, slot_recv, capacity), "tp", axis=1, tiled=True)
    rows = capacity * patches
    grads = routed.reshape(rows, width)
    values = saved_inputs.reshape(rows, width).astype(jnp.float32)
    mean_v = jnp.mean(values, axis=1, keepdims=True)
    var_v = jnp.mean((values - mean_v) ** 2, axis=1, keepdims=True)
    inv_std = 1.0 / jnp.sqrt(var_v + epsilon)
    centred = (values - mean_v) * inv_std
    normed = (centred * norm_gain[None, :]).astype(jnp.bfloat16)
    preact = jnp.dot(normed, up_weight, preferred_element_type=jnp.float32)
    hidden = gelu_value(preact).astype(jnp.bfloat16)
    grad_hidden = jnp.dot(grads, down_weight.T, preferred_element_type=jnp.float32)
    grad_pre = (grad_hidden * gelu_slope(preact)).astype(jnp.bfloat16)
    down_local = jnp.dot(hidden.T, grads, preferred_element_type=jnp.float32)
    up_local = jnp.dot(normed.T, grad_pre, preferred_element_type=jnp.float32)
    partial_normed = jnp.dot(grad_pre, up_weight.T, preferred_element_type=jnp.float32)
    up_grads, down_grads = (
        lax.psum_scatter(
            up_local.astype(jnp.bfloat16), "rep", scatter_dimension=0, tiled=True
        ).astype(jnp.float32),
        lax.psum_scatter(
            down_local.astype(jnp.bfloat16), "rep", scatter_dimension=1, tiled=True
        ).astype(jnp.float32),
    )
    start = lax.axis_index("tp") * slab
    grad_normed = lax.psum(partial_normed.astype(jnp.bfloat16), "tp").astype(jnp.float32)
    gain_grads = lax.psum(jnp.sum(grad_normed * centred, axis=0), "rep")
    scaled = grad_normed * norm_gain[None, :]
    first = jnp.mean(scaled, axis=1, keepdims=True)
    second = jnp.mean(scaled * centred, axis=1, keepdims=True)
    result = grads.astype(jnp.float32) + inv_std * (scaled - first - centred * second)
    result = result.reshape(capacity, patches, width)
    input_grads = lax.dynamic_slice_in_dim(result, start, slab, 1).astype(jnp.bfloat16)
    return (input_grads, up_grads, down_grads, gain_grads)


def solution(mesh):
    in_specs = (
        P("rep", "tp", None),
        P("rep"),
        P("rep"),
        P("rep", None, None),
        P(None, "tp"),
        P("tp", None),
        P(),
    )
    out_specs = (P("rep", "tp", None), P("rep", "tp"), P("tp", "rep"), P())
    return jax.shard_map(local, mesh=mesh, in_specs=in_specs, out_specs=out_specs, check_vma=False)
```

profile of v0, /device:TPU:0, one launch (start us, length us, event | category | flops | bytes accessed | tf_op | source)
XLA Modules:
  0.0 227.4 jit_solution(4812168266985921151)
XLA Ops:
  8.0 0.0 copy-start
  8.0 0.0 copy-start.6
  8.0 0.0 copy-start.4
  8.0 0.0 copy-start.5
  8.0 0.9 fusion.26
  8.9 0.9 select_reduce_fusion
  9.9 0.7 copy.19
  10.5 7.3 %all-to-all-start = ((s32[8,1,1]{2,1,0:T(1,128)}), s32[8,1,1]{2,1,0:T(1,128)S(1)}, u32[]{:S(2)}, u32[]{:S(2)}) async-start(s32[8,1,1]{2,1,0:T(1,128)} %copy.19), calls=%async_computation | async-start | bytes 8192 | tf_op jit(solution)/shard_map/all_to_all | solution.py:53
  17.8 1.4 convert_reduce_fusion
  19.3 0.1 div.18
  19.3 1.6 multiply_reduce_fusion
  20.9 0.1 sqrt.6
  21.0 0.0 copy-done.6
  21.0 0.0 copy-done.4
  21.1 0.3 convolution_convert_fusion.4
  21.4 0.0 copy-done.5
  21.4 2.5 %multiply_convert_fusion.1 = bf16[384,1280]{1,0:T(8,128)(2,1)} fusion(bf16[8,48,1280]{2,1,0:T(8,128)(2,1)} %param.10, f32[1280]{0:T(1024)S(1)} %copy-done.5, f32[384]{0:T(512)S(1)} %div.18, f32[384]{0:T(512)S(1)} %sqrt.6), kind=kLoop, calls=%fused_computation.29 | loop fusion | flops 2457600 | bytes 1974272 | tf_op jit(solution)/shard_map/convert_element_type | solution.py:63
  23.9 0.8 copy.20
  24.7 0.0 all-to-all-done
  24.7 6.0 %all-to-all-start.1 = ((bf16[8,12,1280]{2,1,0:T(8,128)(2,1)}), bf16[8,12,1280]{2,1,0:T(8,128)(2,1)}, u32[]{:S(2)}, u32[]{:S(2)}) async-start(bf16[8,12,1280]{2,1,0:T(8,128)(2,1)} %copy.20), calls=%async_computation.1 | async-start | bytes 655360 | tf_op jit(solution)/shard_map/all_to_all | solution.py:52
  30.7 0.0 all-reduce.2.cloned.1.call-start
  30.7 0.0 copy-done
  30.7 4.0 %fusion.33 = f32[384,1280]{1,0:T(8,128)} fusion(bf16[384,1280]{1,0:T(8,128)(2,1)} %multiply_convert_fusion.1, bf16[1280,1280]{1,0:T(8,128)(2,1)S(1)} %copy-done), kind=kOutput, calls=%fused_computation.56 | convolution fusion | flops 1258291200 | bytes 6225920 | tf_op jit(solution)/shard_map/dot_general | solution.py:64
  34.7 0.2 reduce.2
  34.9 5.6 %all-to-all-done.1 = bf16[8,12,1280]{2,1,0:T(8,128)(2,1)} async-done(((bf16[8,12,1280]{2,1,0:T(8,128)(2,1)}), bf16[8,12,1280]{2,1,0:T(8,128)(2,1)}, u32[]{:S(2)}, u32[]{:S(2)}) %all-to-all-start.1) | async-done | bytes 245792 | tf_op jit(solution)/shard_map/all_to_all | solution.py:52
  40.5 0.0 copy-start.7
  40.5 1.3 convolution_convert_fusion.3
  41.9 9.7 %all_gather.3 = bf16[8,48,1280]{2,0,1:T(8,128)(2,1)S(1)} all-gather(bf16[8,12,1280]{2,0,1:T(8,128)(2,1)S(1)} %convolution_convert_fusion.3), channel_id=1, replica_groups=mesh['rep'=8,'tp'=4] {'tp'}, dimensions={1}, use_global_device_ids=true | all-gather | bytes 1228800 | tf_op jit(solution)/shard_map/all_gather | solution.py:55
  51.5 0.2 copy.22
  51.7 0.0 copy-start.2
  51.7 0.0 copy-done.7
  51.7 3.8 %fusion = bf16[384,1280]{1,0:T(8,128)(2,1)S(1)} fusion(bf16[384,1280]{1,0:T(8,128)(2,1)S(1)} %bitcast.33, bf16[1280,1280]{1,0:T(8,128)(2,1)S(1)} %copy-done.7, f32[384,1280]{1,0:T(8,128)} %fusion.33), kind=kOutput, calls=%fused_computation.5 | convolution fusion | flops 1267630080 | bytes 7208960 | tf_op jit(solution)/shard_map/dot_general | solution.py:66
  55.5 0.0 copy-done.2
  55.6 0.0 copy-start.8
  55.6 0.9 copy-done.8
  56.5 2.4 %convolution_convert_fusion.2 = bf16[384,1280]{1,0:T(8,128)(2,1)} fusion(bf16[384,1280]{1,0:T(8,128)(2,1)S(1)} %fusion, bf16[1280,1280]{1,0:T(8,128)(2,1)S(1)} %copy-done), kind=kOutput, calls=%fused_computation.6 | convolution fusion | flops 1258782720 | bytes 5242880 | tf_op jit(solution)/shard_map/dot_general | solution.py:70
  58.9 0.0 all-reduce.2.cloned.1.call-update
  59.0 0.0 reduce-scatter.3.cloned.1.call-start
  59.0 5.1 %convolution_convert_fusion.1 = bf16[1280,1280]{1,0:T(8,128)(2,1)} fusion(bf16[384,1280]{1,0:T(8,128)(2,1)} %multiply_convert_fusion.1, bf16[384,1280]{1,0:T(8,128)(2,1)} %copy-done.8), kind=kOutput, calls=%fused_computation.1 | convolution fusion | flops 1259929600 | bytes 5242880 | tf_op jit(solution)/shard_map/dot_general | solution.py:69
  64.1 0.0 reduce-scatter.3.cloned.1.call-update
  64.1 0.2 reduce-scatter.5.cloned.1.call-start
  64.4 5.5 %convolution_convert_fusion = bf16[1280,1280]{0,1:T(8,128)(2,1)} fusion(bf16[384,1280]{1,0:T(8,128)(2,1)} %bitcast.34, f32[384,1280]{1,0:T(8,128)} %fusion.33), kind=kOutput, calls=%fused_computation | convolution fusion | flops 1264353280 | bytes 6225920 | tf_op jit(solution)/shard_map/dot_general | solution.py:68
  69.9 0.0 reduce-scatter.5.cloned.1.call-update
  69.9 23.6 %all-reduce.2.cloned.1.call-done = bf16[384,1280]{1,0:T(8,128)(2,1)} async-done(((bf16[384,1280]{1,0:T(8,128)(2,1)}), bf16[384,1280]{1,0:T(8,128)(2,1)}) %all-reduce.2.cloned.1.call-update) | async-done | bytes 983056 | tf_op jit(solution)/shard_map/psum | solution.py:80
  93.5 0.0 copy-start.1
  93.5 0.0 copy-start.3
  93.5 2.6 %fusion.8 = (f32[1280]{0:T(1024)S(1)}, f32[384]{0:T(512)S(1)}, f32[384]{0:T(512)S(1)}) fusion(bf16[384,1280]{1,0:T(8,128)(2,1)} %all-reduce.2.cloned.1.call-done, bf16[8,48,1280]{2,1,0:T(8,128)(2,1)} %param.10, f32[384]{0:T(512)S(1)} %div.18, f32[384]{0:T(512)S(1)} %sqrt.6, f32[1280]{0:T(1024)S(1)} %copy-done.5), kind=kLoop, calls=%fused_computation.18 | loop fusion | flops 4913152 | bytes 1982464 | tf_op jit(solution)/shard_map/reduce_sum | solution.py:81
  96.1 0.0 copy-done.1
  96.1 0.0 copy-done.3
  96.1 2.1 fusion.6
  98.2 0.1 constant_dynamic-slice_fusion
  98.3 0.8 copy.28
  99.0 22.1 %psum.15 = f32[1280]{0:T(1024)} all-reduce(f32[1280]{0:T(1024)S(1)} %get-tuple-element.4), channel_id=1, replica_groups=mesh['rep'=8,'tp'=4] {'rep'}, use_global_device_ids=true, to_apply=%region_10.11 | all-reduce | flops 1280 | bytes 10240 | tf_op jit(solution)/shard_map/psum | solution.py:81
  121.2 18.0 %reduce-scatter.3.cloned.1.call-done = bf16[160,1280]{1,0:T(8,128)(2,1)} async-done(((bf16[1280,1280]{1,0:T(8,128)(2,1)}), bf16[160,1280]{1,0:T(8,128)(2,1)}) %reduce-scatter.3.cloned.1.call-update) | async-done | bytes 409616 | tf_op jit(solution)/shard_map/reduce_scatter | solution.py:72
  139.2 1.9 convert_element_type.63
  141.1 76.9 %reduce-scatter.5.cloned.1.call-done = bf16[1280,160]{0,1:T(8,128)(2,1)} async-done(((bf16[1280,1280]{0,1:T(8,128)(2,1)}), bf16[1280,160]{0,1:T(8,128)(2,1)}) %reduce-scatter.5.cloned.1.call-update) | async-done | bytes 409616 | tf_op jit(solution)/shard_map/reduce_scatter | solution.py:75
  218.0 1.9 convert_element_type.66
  (4 shorter events, 0.0 us)
Async XLA Ops:
  8.0 22.7 %copy-start = (bf16[1280,1280]{1,0:T(8,128)(2,1)S(1)}, bf16[1280,1280]{1,0:T(8,128)(2,1)}, u32[]{:S(2)}) copy-start(bf16[1280,1280]{1,0:T(8,128)(2,1)} %param.11) | copy-start | bytes 9830404
  8.0 13.0 %copy-start.6 = (s32[4]{0:T(128)S(1)}, s32[4]{0:T(128)}, u32[]{:S(2)}) copy-start(s32[4]{0:T(128)} %param.8) | copy-start | bytes 52
  8.0 13.0 %copy-start.4 = (bf16[4,12,1280]{2,0,1:T(4,128)(2,1)S(1)}, bf16[4,12,1280]{2,0,1:T(4,128)(2,1)}, u32[]{:S(2)}) copy-start(bf16[4,12,1280]{2,0,1:T(4,128)(2,1)} %param.7) | copy-start | bytes 368644
  8.0 13.4 %copy-start.5 = (f32[1280]{0:T(1024)S(1)}, f32[1280]{0:T(1024)}, u32[]{:S(2)}) copy-start(f32[1280]{0:T(1024)} %param.13) | copy-start | bytes 15364
  10.5 14.2 %all-to-all-start = ((s32[8,1,1]{2,1,0:T(1,128)}), s32[8,1,1]{2,1,0:T(1,128)S(1)}, u32[]{:S(2)}, u32[]{:S(2)}) async-start(s32[8,1,1]{2,1,0:T(1,128)} %copy.19), calls=%async_computation | async-start | bytes 8192 | tf_op jit(solution)/shard_map/all_to_all | solution.py:53
  24.7 15.8 %all-to-all-start.1 = ((bf16[8,12,1280]{2,1,0:T(8,128)(2,1)}), bf16[8,12,1280]{2,1,0:T(8,128)(2,1)}, u32[]{:S(2)}, u32[]{:S(2)}) async-start(bf16[8,12,1280]{2,1,0:T(8,128)(2,1)} %copy.20), calls=%async_computation.1 | async-start | bytes 655360 | tf_op jit(solution)/shard_map/all_to_all | solution.py:52
  30.7 62.8 %all-reduce.2.cloned.1.call-start = ((), (), s32[]{:S(2)}) async-start(), calls=%async_computation.4 | async-start | bytes 1966080 | tf_op jit(solution)/shard_map/psum | solution.py:80
  40.5 11.2 %copy-start.7 = (bf16[1280,1280]{1,0:T(8,128)(2,1)S(1)}, bf16[1280,1280]{1,0:T(8,128)(2,1)}, u32[]{:S(2)}) copy-start(bf16[1280,1280]{1,0:T(8,128)(2,1)} %param.12) | copy-start | bytes 9830404
  51.7 3.9 %copy-start.2 = (bf16[8,48,1280]{2,1,0:T(8,128)(2,1)}, bf16[8,48,1280]{2,1,0:T(8,128)(2,1)S(1)}, u32[]{:S(2)}) copy-start(bf16[8,48,1280]{2,1,0:T(8,128)(2,1)S(1)} %copy.22) | copy-start | bytes 2949124
  55.6 1.0 copy-start.8
  59.0 80.2 %reduce-scatter.3.cloned.1.call-start = ((), (), s32[]{:S(2)}) async-start(), calls=%async_computation.5 | async-start | bytes 3686400 | tf_op jit(solution)/shard_map/reduce_scatter | solution.py:72
  64.1 153.9 %reduce-scatter.5.cloned.1.call-start = ((), (), s32[]{:S(2)}) async-start(), calls=%async_computation.6 | async-start | bytes 3686400 | tf_op jit(solution)/shard_map/reduce_scatter | solution.py:75
  93.5 2.6 %copy-start.1 = (bf16[8,48,1280]{2,1,0:T(8,128)(2,1)S(1)}, bf16[8,48,1280]{2,1,0:T(8,128)(2,1)}, u32[]{:S(2)}) copy-start(bf16[8,48,1280]{2,1,0:T(8,128)(2,1)} %param.10) | copy-start | bytes 2949124
  93.5 2.6 %copy-start.3 = (bf16[8,48,1280]{2,1,0:T(8,128)(2,1)S(1)}, bf16[8,48,1280]{2,1,0:T(8,128)(2,1)}, u32[]{:S(2)}) copy-start(bf16[8,48,1280]{2,1,0:T(8,128)(2,1)} %copy-done.2) | copy-start | bytes 2949124
Sparse Core Ops, SparseCore 0:
  59.1 34.3 all-reduce.1
Sparse Core Ops, SparseCore 1:
  64.2 74.9 reduce-scatter.2
  142.6 75.3 reduce-scatter.4
where the time goes:
time: 228 us; the launch traced here: 227 us
  waiting for transfers between devices  124 us (54%)
  blocking collectives  31.8 us (14%)
  matrix products  22.5 us (10%)
  other arithmetic  16.1 us (7%)
  between operations  15.7 us (7%)
  starting transfers between devices  13.6 us (6%)
  local copies, waits for them, and re-layouts  3.62 us (2%)
    reduce_scatter x1, waiting for transfers between devices, local(): lax.psum_scatter(down_local.astype(jnp.bfloat16), 'rep', scatter_dimensio...  76.9 us
    psum x1, waiting for transfers between devices, local(): lax.psum(partial_normed.astype(jnp.bfloat16), 'tp').astype(jnp.float32)  23.6 us
    psum x1, blocking collectives, local(): gain_grads = lax.psum(jnp.sum(grad_normed * centred, axis=0), 'rep')  22.1 us
    reduce_scatter x1, waiting for transfers between devices, local(): lax.psum_scatter(up_local.astype(jnp.bfloat16), 'rep', scatter_dimension=...  18 us
    all_gather x1, blocking collectives, local(): lax.all_gather(compact(inbound, slot_recv, capacity), 'tp', axis=1, tiled...  9.67 us
    all_to_all x1, starting transfers between devices, local(): lax.all_to_all(slot_sent, 'rep', split_axis=0, concat_axis=0, tiled=True)  7.31 us
    all_to_all x1, starting transfers between devices, local(): lax.all_to_all(packed, 'rep', split_axis=0, concat_axis=0, tiled=True)  6 us
    all_to_all x1, waiting for transfers between devices, local(): lax.all_to_all(packed, 'rep', split_axis=0, concat_axis=0, tiled=True)  5.58 us
  transfers between devices with their start and end apart: 5, of which 4 were waited for; matrix products, arithmetic and copies ran while one was open for 13% of the time, Pallas kernels for 0%

commit v1 on v0

--- a/solution.py
+++ b/solution.py
@@ -78,7 +78,7 @@
     )
     start = lax.axis_index("tp") * slab
     grad_normed = lax.psum(partial_normed.astype(jnp.bfloat16), "tp").astype(jnp.float32)
-    gain_grads = lax.psum(jnp.sum(grad_normed * centred, axis=0), "rep")
+    gain_grads = jnp.sum(lax.all_gather(jnp.sum(grad_normed * centred, axis=0), "rep"), axis=0)
     scaled = grad_normed * norm_gain[None, :]
     first = jnp.mean(scaled, axis=1, keepdims=True)
     second = jnp.mean(scaled * centred, axis=1, keepdims=True)

time: 228 us -> 228 us (level)
  waiting for transfers between devices: 124 us -> 115 us
  blocking collectives: 31.8 us -> 40.6 us
    all_gather x0 -> x1, blocking collectives: none -> 30.9 us  [local(): lax.all_gather(jnp.sum(grad_normed * centred, axis=0), 'rep')]
    psum x1 -> x0, blocking collectives: 22.1 us -> none  [local(): gain_grads = lax.psum(jnp.sum(grad_normed * centred, axis=0), 'rep')]
    reduce_scatter x1, waiting for transfers between devices: 18 us -> 8.42 us  [local(): lax.psum_scatter(up_local.astype(jnp.bfloat16), 'rep', scatter_dimension=...]
where the time goes in v1:
time: 228 us; the launch traced here: 227 us
  waiting for transfers between devices  115 us (50%)
  blocking collectives  40.6 us (18%)
  matrix products  22.5 us (10%)
  other arithmetic  16.7 us (7%)
  between operations  15.7 us (7%)
  starting transfers between devices  13.6 us (6%)
  local copies, waits for them, and re-layouts  3.63 us (2%)
    reduce_scatter x1, waiting for transfers between devices, local(): lax.psum_scatter(down_local.astype(jnp.bfloat16), 'rep', scatter_dimensio...  77 us
    all_gather x1, blocking collectives, local(): lax.all_gather(jnp.sum(grad_normed * centred, axis=0), 'rep')  30.9 us
    psum x1, waiting for transfers between devices, local(): lax.psum(partial_normed.astype(jnp.bfloat16), 'tp').astype(jnp.float32)  23.6 us
    all_gather x1, blocking collectives, local(): lax.all_gather(compact(inbound, slot_recv, capacity), 'tp', axis=1, tiled...  9.67 us
    reduce_scatter x1, waiting for transfers between devices, local(): lax.psum_scatter(up_local.astype(jnp.bfloat16), 'rep', scatter_dimension=...  8.42 us
    all_to_all x1, starting transfers between devices, local(): lax.all_to_all(slot_sent, 'rep', split_axis=0, concat_axis=0, tiled=True)  7.31 us
    all_to_all x1, starting transfers between devices, local(): lax.all_to_all(packed, 'rep', split_axis=0, concat_axis=0, tiled=True)  6 us
    all_to_all x1, waiting for transfers between devices, local(): lax.all_to_all(packed, 'rep', split_axis=0, concat_axis=0, tiled=True)  5.58 us
  transfers between devices with their start and end apart: 5, of which 4 were waited for; matrix products, arithmetic and copies ran while one was open for 13% of the time, Pallas kernels for 0%

profile of v1, /device:TPU:0, one launch (start us, length us, event | category | flops | bytes accessed | tf_op | source)
XLA Modules:
  0.0 227.4 jit_solution(13557352704063759172)
XLA Ops:
  8.0 0.0 copy-start
  8.0 0.0 copy-start.6
  8.0 0.0 copy-start.4
  8.0 0.0 copy-start.5
  8.0 0.9 fusion.26
  8.9 0.9 select_reduce_fusion
  9.9 0.7 copy.19
  10.5 7.3 %all-to-all-start = ((s32[8,1,1]{2,1,0:T(1,128)}), s32[8,1,1]{2,1,0:T(1,128)S(1)}, u32[]{:S(2)}, u32[]{:S(2)}) async-start(s32[8,1,1]{2,1,0:T(1,128)} %copy.19), calls=%async_computation | async-start | bytes 8192 | tf_op jit(solution)/shard_map/all_to_all | solution.py:53
  17.8 1.4 convert_reduce_fusion
  19.3 0.1 div.18
  19.3 1.6 multiply_reduce_fusion
  20.9 0.1 sqrt.6
  21.0 0.0 copy-done.6
  21.0 0.0 copy-done.4
  21.1 0.3 convolution_convert_fusion.4
  21.4 0.0 copy-done.5
  21.4 2.5 %multiply_convert_fusion.1 = bf16[384,1280]{1,0:T(8,128)(2,1)} fusion(bf16[8,48,1280]{2,1,0:T(8,128)(2,1)} %param.10, f32[1280]{0:T(1024)S(1)} %copy-done.5, f32[384]{0:T(512)S(1)} %div.18, f32[384]{0:T(512)S(1)} %sqrt.6), kind=kLoop, calls=%fused_computation.29 | loop fusion | flops 2457600 | bytes 1974272 | tf_op jit(solution)/shard_map/convert_element_type | solution.py:63
  23.9 0.8 copy.20
  24.7 0.0 all-to-all-done
  24.7 6.0 %all-to-all-start.1 = ((bf16[8,12,1280]{2,1,0:T(8,128)(2,1)}), bf16[8,12,1280]{2,1,0:T(8,128)(2,1)}, u32[]{:S(2)}, u32[]{:S(2)}) async-start(bf16[8,12,1280]{2,1,0:T(8,128)(2,1)} %copy.20), calls=%async_computation.1 | async-start | bytes 655360 | tf_op jit(solution)/shard_map/all_to_all | solution.py:52
  30.7 0.0 all-reduce.2.cloned.1.call-start
  30.7 0.0 copy-done
  30.7 4.0 %fusion.33 = f32[384,1280]{1,0:T(8,128)} fusion(bf16[384,1280]{1,0:T(8,128)(2,1)} %multiply_convert_fusion.1, bf16[1280,1280]{1,0:T(8,128)(2,1)S(1)} %copy-done), kind=kOutput, calls=%fused_computation.56 | convolution fusion | flops 1258291200 | bytes 6225920 | tf_op jit(solution)/shard_map/dot_general | solution.py:64
  34.7 0.2 reduce.3
  34.9 5.6 %all-to-all-done.1 = bf16[8,12,1280]{2,1,0:T(8,128)(2,1)} async-done(((bf16[8,12,1280]{2,1,0:T(8,128)(2,1)}), bf16[8,12,1280]{2,1,0:T(8,128)(2,1)}, u32[]{:S(2)}, u32[]{:S(2)}) %all-to-all-start.1) | async-done | bytes 245792 | tf_op jit(solution)/shard_map/all_to_all | solution.py:52
  40.5 0.0 copy-start.7
  40.5 1.3 convolution_convert_fusion.3
  41.9 9.7 %all_gather.9 = bf16[8,48,1280]{2,0,1:T(8,128)(2,1)S(1)} all-gather(bf16[8,12,1280]{2,0,1:T(8,128)(2,1)S(1)} %convolution_convert_fusion.3), channel_id=1, replica_groups=mesh['rep'=8,'tp'=4] {'tp'}, dimensions={1}, use_global_device_ids=true | all-gather | bytes 1228800 | tf_op jit(solution)/shard_map/all_gather | solution.py:55
  51.5 0.2 copy.22
  51.7 0.0 copy-start.2
  51.7 0.0 copy-done.7
  51.7 3.8 %fusion = bf16[384,1280]{1,0:T(8,128)(2,1)S(1)} fusion(bf16[384,1280]{1,0:T(8,128)(2,1)S(1)} %bitcast.33, bf16[1280,1280]{1,0:T(8,128)(2,1)S(1)} %copy-done.7, f32[384,1280]{1,0:T(8,128)} %fusion.33), kind=kOutput, calls=%fused_computation.5 | convolution fusion | flops 1267630080 | bytes 7208960 | tf_op jit(solution)/shard_map/dot_general | solution.py:66
  55.5 0.0 copy-done.2
  55.6 0.0 copy-start.8
  55.6 0.9 copy-done.8
  56.5 2.4 %convolution_convert_fusion.2 = bf16[384,1280]{1,0:T(8,128)(2,1)} fusion(bf16[384,1280]{1,0:T(8,128)(2,1)S(1)} %fusion, bf16[1280,1280]{1,0:T(8,128)(2,1)S(1)} %copy-done), kind=kOutput, calls=%fused_computation.6 | convolution fusion | flops 1258782720 | bytes 5242880 | tf_op jit(solution)/shard_map/dot_general | solution.py:70
  58.9 0.0 all-reduce.2.cloned.1.call-update
  59.0 0.0 reduce-scatter.3.cloned.1.call-start
  59.0 5.1 %convolution_convert_fusion.1 = bf16[1280,1280]{1,0:T(8,128)(2,1)} fusion(bf16[384,1280]{1,0:T(8,128)(2,1)} %multiply_convert_fusion.1, bf16[384,1280]{1,0:T(8,128)(2,1)} %copy-done.8), kind=kOutput, calls=%fused_computation.1 | convolution fusion | flops 1259929600 | bytes 5242880 | tf_op jit(solution)/shard_map/dot_general | solution.py:69
  64.1 0.0 reduce-scatter.3.cloned.1.call-update
  64.1 0.2 reduce-scatter.5.cloned.1.call-start
  64.4 5.5 %convolution_convert_fusion = bf16[1280,1280]{0,1:T(8,128)(2,1)} fusion(bf16[384,1280]{1,0:T(8,128)(2,1)} %bitcast.34, f32[384,1280]{1,0:T(8,128)} %fusion.33), kind=kOutput, calls=%fused_computation | convolution fusion | flops 1264353280 | bytes 6225920 | tf_op jit(solution)/shard_map/dot_general | solution.py:68
  69.9 0.0 reduce-scatter.5.cloned.1.call-update
  69.9 23.6 %all-reduce.2.cloned.1.call-done = bf16[384,1280]{1,0:T(8,128)(2,1)} async-done(((bf16[384,1280]{1,0:T(8,128)(2,1)}), bf16[384,1280]{1,0:T(8,128)(2,1)}) %all-reduce.2.cloned.1.call-update) | async-done | bytes 983056 | tf_op jit(solution)/shard_map/psum | solution.py:80
  93.5 0.0 copy-start.1
  93.5 0.0 copy-start.3
  93.5 2.6 %fusion.8 = (f32[1280]{0:T(1024)S(1)}, f32[384]{0:T(512)S(1)}, f32[384]{0:T(512)S(1)}) fusion(bf16[384,1280]{1,0:T(8,128)(2,1)} %all-reduce.2.cloned.1.call-done, bf16[8,48,1280]{2,1,0:T(8,128)(2,1)} %param.10, f32[384]{0:T(512)S(1)} %div.18, f32[384]{0:T(512)S(1)} %sqrt.6, f32[1280]{0:T(1024)S(1)} %copy-done.5), kind=kLoop, calls=%fused_computation.18 | loop fusion | flops 4913152 | bytes 1982464 | tf_op jit(solution)/shard_map/reduce_sum | solution.py:81
  96.1 0.0 copy-done.1
  96.1 0.0 copy-done.3
  96.1 2.1 fusion.6
  98.2 0.1 constant_dynamic-slice_fusion
  98.3 0.8 copy.28
  99.1 30.9 %all-gather.1 = f32[8,1,1280]{2,1,0:T(1,128)S(1)} all-gather(f32[1,1,1280]{2,1,0:T(1,128)S(1)} %reshape.87), channel_id=2, replica_groups=mesh['rep'=8,'tp'=4] {'rep'}, dimensions={0}, use_global_device_ids=true | all-gather | bytes 46080 | tf_op jit(solution)/shard_map/all_gather | solution.py:81
  130.0 0.6 reduce_sum.69
  130.6 8.4 %reduce-scatter.3.cloned.1.call-done = bf16[160,1280]{1,0:T(8,128)(2,1)} async-done(((bf16[1280,1280]{1,0:T(8,128)(2,1)}), bf16[160,1280]{1,0:T(8,128)(2,1)}) %reduce-scatter.3.cloned.1.call-update) | async-done | bytes 409616 | tf_op jit(solution)/shard_map/reduce_scatter | solution.py:72
  139.0 1.9 convert_element_type.63
  141.0 77.0 %reduce-scatter.5.cloned.1.call-done = bf16[1280,160]{0,1:T(8,128)(2,1)} async-done(((bf16[1280,1280]{0,1:T(8,128)(2,1)}), bf16[1280,160]{0,1:T(8,128)(2,1)}) %reduce-scatter.5.cloned.1.call-update) | async-done | bytes 409616 | tf_op jit(solution)/shard_map/reduce_scatter | solution.py:75
  218.0 1.9 convert_element_type.66
  (5 shorter events, 0.0 us)
Async XLA Ops:
  8.0 22.7 %copy-start = (bf16[1280,1280]{1,0:T(8,128)(2,1)S(1)}, bf16[1280,1280]{1,0:T(8,128)(2,1)}, u32[]{:S(2)}) copy-start(bf16[1280,1280]{1,0:T(8,128)(2,1)} %param.11) | copy-start | bytes 9830404
  8.0 13.0 %copy-start.6 = (s32[4]{0:T(128)S(1)}, s32[4]{0:T(128)}, u32[]{:S(2)}) copy-start(s32[4]{0:T(128)} %param.8) | copy-start | bytes 52
  8.0 13.0 %copy-start.4 = (bf16[4,12,1280]{2,0,1:T(4,128)(2,1)S(1)}, bf16[4,12,1280]{2,0,1:T(4,128)(2,1)}, u32[]{:S(2)}) copy-start(bf16[4,12,1280]{2,0,1:T(4,128)(2,1)} %param.7) | copy-start | bytes 368644
  8.0 13.4 %copy-start.5 = (f32[1280]{0:T(1024)S(1)}, f32[1280]{0:T(1024)}, u32[]{:S(2)}) copy-start(f32[1280]{0:T(1024)} %param.13) | copy-start | bytes 15364
  10.5 14.2 %all-to-all-start = ((s32[8,1,1]{2,1,0:T(1,128)}), s32[8,1,1]{2,1,0:T(1,128)S(1)}, u32[]{:S(2)}, u32[]{:S(2)}) async-start(s32[8,1,1]{2,1,0:T(1,128)} %copy.19), calls=%async_computation | async-start | bytes 8192 | tf_op jit(solution)/shard_map/all_to_all | solution.py:53
  24.7 15.8 %all-to-all-start.1 = ((bf16[8,12,1280]{2,1,0:T(8,128)(2,1)}), bf16[8,12,1280]{2,1,0:T(8,128)(2,1)}, u32[]{:S(2)}, u32[]{:S(2)}) async-start(bf16[8,12,1280]{2,1,0:T(8,128)(2,1)} %copy.20), calls=%async_computation.1 | async-start | bytes 655360 | tf_op jit(solution)/shard_map/all_to_all | solution.py:52
  30.7 62.8 %all-reduce.2.cloned.1.call-start = ((), (), s32[]{:S(2)}) async-start(), calls=%async_computation.4 | async-start | bytes 1966080 | tf_op jit(solution)/shard_map/psum | solution.py:80
  40.5 11.2 %copy-start.7 = (bf16[1280,1280]{1,0:T(8,128)(2,1)S(1)}, bf16[1280,1280]{1,0:T(8,128)(2,1)}, u32[]{:S(2)}) copy-start(bf16[1280,1280]{1,0:T(8,128)(2,1)} %param.12) | copy-start | bytes 9830404
  51.7 3.9 %copy-start.2 = (bf16[8,48,1280]{2,1,0:T(8,128)(2,1)}, bf16[8,48,1280]{2,1,0:T(8,128)(2,1)S(1)}, u32[]{:S(2)}) copy-start(bf16[8,48,1280]{2,1,0:T(8,128)(2,1)S(1)} %copy.22) | copy-start | bytes 2949124
  55.6 1.0 copy-start.8
  59.0 80.1 %reduce-scatter.3.cloned.1.call-start = ((), (), s32[]{:S(2)}) async-start(), calls=%async_computation.5 | async-start | bytes 3686400 | tf_op jit(solution)/shard_map/reduce_scatter | solution.py:72
  64.1 153.9 %reduce-scatter.5.cloned.1.call-start = ((), (), s32[]{:S(2)}) async-start(), calls=%async_computation.6 | async-start | bytes 3686400 | tf_op jit(solution)/shard_map/reduce_scatter | solution.py:75
  93.5 2.6 %copy-start.1 = (bf16[8,48,1280]{2,1,0:T(8,128)(2,1)S(1)}, bf16[8,48,1280]{2,1,0:T(8,128)(2,1)}, u32[]{:S(2)}) copy-start(bf16[8,48,1280]{2,1,0:T(8,128)(2,1)} %param.10) | copy-start | bytes 2949124
  93.5 2.6 %copy-start.3 = (bf16[8,48,1280]{2,1,0:T(8,128)(2,1)S(1)}, bf16[8,48,1280]{2,1,0:T(8,128)(2,1)}, u32[]{:S(2)}) copy-start(bf16[8,48,1280]{2,1,0:T(8,128)(2,1)} %copy-done.2) | copy-start | bytes 2949124
Sparse Core Ops, SparseCore 0:
  59.1 34.3 all-reduce.1
Sparse Core Ops, SparseCore 1:
  64.2 74.8 reduce-scatter.2
  142.5 75.4 reduce-scatter.4
